TPU v7x, 256 devices: a whole 4x4x8 slice. The times are simulated.
256 devices in a mesh: chan: 64 (over y, x_lo, z), rep: 4 (over x_hi, core).
Axes of the slice: x: 4 (x_hi: 2, x_lo: 2; x = x_hi * 2 + x_lo), y: 4, z: 8, core: 2. Of those that a mesh axis runs over, the one named last changes fastest.
Arguments:
- records: bfloat16 [2, 64, 256, 2048], P(None, None, 'rep', 'chan'), may hold values from -6 to 6
- sources: int32 [128], replicated, may hold values from 0 to 16383
- dead_list: int32 [2, 1024], replicated, may hold values from 0 to 16383
Outputs:
- correlations: float32 [128, 64, 16384], P('rep', None, 'chan')
All inputs are finite; a program needn't handle non-finite values.
Results may differ from a plain program's by a relative error of at most 0.0072.
Values may be sent and summed in bfloat16 or wider, within the bound.
A program may use at most 64 MiB of HBM per device.

v0:
```python
import math
import jax
import jax.numpy as jnp
from jax import lax
from jax.sharding import PartitionSpec as P

WINDOW_SAMPLES = 2048
K = 256
K0 = 16
HALF = 32
WH = 32
LAGS = 64
tile_span = 128
tiny_eps = 1e-06


def live_table(dead_list, total):
    window_count, listed = dead_list.shape
    window_rows = jnp.broadcast_to(
        jnp.arange(window_count, dtype=jnp.int32)[:, None], (window_count, listed)
    )
    return jnp.ones((window_count, total), jnp.float32).at[window_rows, dead_list].set(0.0)


def running_mean(records):
    length = records.shape[-1]
    blocks = length // tile_span
    leading = records.shape[:-1]
    magnitude = jnp.abs(records)
    padded = jnp.pad(magnitude, [(0, 0)] * (records.ndim - 1) + [(tile_span, tile_span)])
    before = padded[..., :length].reshape(leading + (blocks, tile_span))
    middle = magnitude.reshape(leading + (blocks, tile_span))
    after = padded[..., 2 * tile_span :].reshape(leading + (blocks, tile_span))
    views = jnp.concatenate([before, middle, after], axis=-1).reshape(-1, 3 * tile_span)
    offsets = jnp.arange(3 * tile_span, dtype=jnp.int32)[:, None] - tile_span
    targets = jnp.arange(tile_span, dtype=jnp.int32)[None, :]
    band_unit_mask = (jnp.abs(offsets - targets) <= HALF).astype(jnp.bfloat16)
    totals = jnp.dot(views, band_unit_mask, preferred_element_type=jnp.float32).reshape(
        leading + (length,)
    )
    sample = jnp.arange(length, dtype=jnp.int32)
    counts = (jnp.minimum(sample, HALF) + jnp.minimum(length - 1 - sample, HALF) + 1).astype(
        jnp.float32
    )
    return totals / counts


def dft_table(length):
    sample = jnp.arange(length, dtype=jnp.int32)[:, None]
    bin_index = K0 + jnp.arange(K, dtype=jnp.int32)[None, :]
    phase = sample * bin_index % length
    angle = phase.astype(jnp.float32) * (2.0 * math.pi / length)
    return jnp.concatenate([jnp.cos(angle), -jnp.sin(angle)], axis=1).astype(jnp.bfloat16)


def whiten(spectrum):
    real_part = spectrum[:, :K]
    imag_part = spectrum[:, K:]
    amplitude = jnp.sqrt(real_part * real_part + imag_part * imag_part)
    index_row = jnp.arange(K, dtype=jnp.int32)[:, None]
    index_col = jnp.arange(K, dtype=jnp.int32)[None, :]
    band = (jnp.abs(index_row - index_col) <= WH).astype(jnp.float32)
    smoothed_amplitude = jnp.dot(amplitude, band, precision=lax.Precision.HIGHEST) / jnp.sum(
        band, axis=0
    )
    return (
        spectrum / (jnp.concatenate([smoothed_amplitude, smoothed_amplitude], axis=1) + tiny_eps)
    ).astype(jnp.bfloat16)


def preprocess(records):
    mean_abs = running_mean(records)
    normed = (records.astype(jnp.float32) / (mean_abs + tiny_eps)).astype(jnp.bfloat16)
    spectrum = jnp.dot(normed, dft_table(records.shape[-1]), preferred_element_type=jnp.float32)
    return whiten(spectrum)


def lag_kernel(source_spectrum):
    bin_index = K0 + jnp.arange(K, dtype=jnp.int32)[None, :]
    lag_index = jnp.arange(LAGS, dtype=jnp.int32)[:, None] - LAGS // 2
    phase = jnp.mod(lag_index * bin_index, WINDOW_SAMPLES)
    angle = phase.astype(jnp.float32) * (2.0 * math.pi / WINDOW_SAMPLES)
    cosine_lookup = jnp.cos(angle)[None, :, None, :]
    sin_table = jnp.sin(angle)[None, :, None, :]
    real_part = source_spectrum[:, None, :, :K].astype(jnp.float32)
    imag_part = source_spectrum[:, None, :, K:].astype(jnp.float32)
    with_real = real_part * cosine_lookup + imag_part * sin_table
    with_imag = imag_part * cosine_lookup - real_part * sin_table
    return jnp.concatenate([with_real, with_imag], axis=3).astype(jnp.bfloat16)


def correlate(kernel, spectra, source_live, chan_live):
    summed = lax.dot_general(
        kernel, spectra, (((2, 3), (0, 2)), ((), ())), preferred_element_type=jnp.float32
    )
    pairs = jnp.dot(source_live.T, chan_live, precision=lax.Precision.HIGHEST)
    return summed / (math.sqrt(K) * jnp.maximum(pairs, 1.0))[:, None, :]


def shards(records, sources, dead_list):
    window_count, groups, ch_width, span_len = records.shape
    reps = lax.axis_size("rep")
    chan_place = lax.axis_index("chan")
    rep_place = lax.axis_index("rep")
    group_share = ch_width * reps
    total = groups * group_share
    live = live_table(dead_list, total)
    group_ids = (
        jnp.arange(groups, dtype=jnp.int32)[:, None] * group_share
        + rep_place * ch_width
        + jnp.arange(ch_width, dtype=jnp.int32)[None, :]
    )
    live_here = live[:, group_ids]
    masked = jnp.where(live_here[..., None] > 0.5, records, jnp.zeros_like(records))
    arrived = lax.all_to_all(masked, "chan", split_axis=1, concat_axis=3, tiled=True)
    flat_rows = arrived.reshape(-1, arrived.shape[-1])
    spectra = preprocess(flat_rows).reshape(arrived.shape[0], ch_width, 2 * K)
    own_ids = (
        chan_place * group_share + rep_place * ch_width + jnp.arange(ch_width, dtype=jnp.int32)
    )
    onehot = (sources[:, None] == own_ids[None, :]).astype(jnp.bfloat16)
    picked = jnp.einsum("sc,wcf->swf", onehot, spectra, preferred_element_type=jnp.float32)
    quarter = sources.shape[0] // reps
    summed = lax.psum(picked, ("chan", "rep"))
    mine = lax.dynamic_slice_in_dim(summed, rep_place * quarter, quarter, 0)
    source_spectrum = mine.astype(jnp.bfloat16)
    source_live = live[:, sources]
    kernel = lag_kernel(source_spectrum)
    quarter_live = lax.dynamic_slice_in_dim(source_live, rep_place * quarter, quarter, 1)
    piece = lax.all_gather(spectra, "rep", axis=1, tiled=True)
    piece_ids = chan_place * group_share + jnp.arange(piece.shape[1], dtype=jnp.int32)
    return correlate(kernel, piece, quarter_live, live[:, piece_ids])


def solution(mesh):
    placed = (P(None, None, "rep", "chan"), P(), P())
    return jax.shard_map(
        shards, mesh=mesh, in_specs=placed, out_specs=P("rep", None, "chan"), check_vma=False
    )
```

profile of v0, /device:TPU:1, one launch (start us, length us, event | category | flops | bytes accessed | tf_op | source)
XLA Modules:
  0.0 189.5 jit_solution(2742913124565968528)
XLA Ops:
  0.0 0.7 fusion.51
  0.7 0.8 and_reduce_fusion
  1.5 0.7 multiply_reduce_fusion
  2.4 8.1 %scatter_custom_fusion = f32[32768]{0:T(1024)S(1)} fusion(s32[2048]{0:T(1024)S(1)} %bitcast.50, f32[2048]{0:T(1024)S(1)} %broadcast.257, f32[]{:T(128)} %constant.27.clone.1), kind=kCustom, calls=%fused_computation.68 | custom fusion | bytes 131076
  10.6 5.0 %copy.42 = f32[2,16384]{0,1:T(8,128)} copy(f32[2,16384]{1,0:T(2,128)S(1)} %reshape.212) | data formatting | bytes 262144 | tf_op jit(solution)/shard_map/scatter | solution.py:22
  15.6 14.1 %gather_fusion = f32[4096,2]{1,0:T(8,128)S(1)} fusion(f32[2,16384]{0,1:T(8,128)} %copy.42, s32[4096]{0:T(1024)S(1)} %broadcast_clamp_fusion), kind=kCustom, calls=%fused_computation | custom fusion | bytes 81920 | tf_op jit(solution)/shard_map/gather | solution.py:113
  30.0 0.7 copy.43
  30.7 1.4 fusion.59
  32.1 1.5 reshape.254
  33.6 13.8 %all-to-all-start = ((bf16[64,2,2048]{2,1,0:T(2,128)(2,1)}), bf16[64,2,2048]{2,1,0:T(2,128)(2,1)S(1)}, u32[]{:S(2)}, u32[]{:S(2)}) async-start(bf16[64,2,2048]{2,1,0:T(2,128)(2,1)} %reshape.254), calls=%async_computation | async-start | bytes 1048576 | tf_op jit(solution)/shard_map/all_to_all | solution.py:115
  47.6 4.0 %gather_fusion.1 = f32[128,2]{1,0:T(8,128)S(1)} fusion(f32[2,16384]{0,1:T(8,128)} %copy.42, s32[1024]{0:T(1024)S(1)} %pad_clamp_fusion.1), kind=kCustom, calls=%fused_computation.1 | custom fusion | bytes 2560 | tf_op jit(solution)/shard_map/gather | solution.py:127
  51.6 4.1 %gather_fusion.2 = f32[256,2]{1,0:T(8,128)S(1)} fusion(f32[2,16384]{0,1:T(8,128)} %copy.42, s32[1024]{0:T(1024)S(1)} %pad_clamp_fusion), kind=kCustom, calls=%fused_computation.2 | custom fusion | bytes 5120 | tf_op jit(solution)/shard_map/gather | solution.py:132
  56.3 9.4 %cosine_convert_fusion = (bf16[2048,256]{1,0:T(8,128)(2,1)}, bf16[2048,256]{1,0:T(8,128)(2,1)}) fusion(s32[256]{0:T(256)S(1)} %iota_add_fusion.1), kind=kLoop, calls=%fused_computation.23 | loop fusion | flops 8912896 | bytes 2098176 | tf_op jit(solution)/shard_map/convert.5
  65.7 0.7 reshape.255
  66.4 1.5 abs_bitcast_fusion
  67.9 2.1 %copy.46 = bf16[2,1,64,64,32]{2,0,4,3,1:T(2,128)(2,1)} copy(bf16[2,1,64,64,32]{2,4,0,3,1:T(8,128)(2,1)S(1)} %get-tuple-element.5) | data formatting | bytes 1048576 | tf_op jit(solution)/shard_map/abs | solution.py:29
  70.0 3.2 %copy.48 = bf16[2,1,64,64,32]{4,3,2,0,1:T(8,128)(2,1)S(1)} copy(bf16[2,1,64,64,32]{2,4,0,3,1:T(8,128)(2,1)S(1)} %get-tuple-element.5) | data formatting | bytes 1048576 | tf_op jit(solution)/shard_map/abs | solution.py:29
  73.2 4.9 %copy.45 = f32[2,1,64,64,32]{2,0,4,3,1:T(2,128)} copy(f32[2,1,64,64,32]{2,4,0,3,1:T(8,128)} %get-tuple-element.6) | data formatting | bytes 2097152 | tf_op jit(solution)/shard_map/convert_element_type | solution.py:73
  78.1 3.4 %reshape.213 = f32[128,2048]{0,1:T(8,128)} reshape(f32[2,1,64,64,32]{2,0,4,3,1:T(2,128)} %copy.45) | data formatting | bytes 2097152 | tf_op jit(solution)/shard_map/convert_element_type | solution.py:73
  81.5 1.3 abs.30
  82.8 1.2 pad_slice_fusion.1
  84.0 1.0 copy.47
  85.0 2.1 %concatenate.23 = bf16[2048,128]{1,0:T(8,128)(2,1)} reshape(bf16[128,2048]{1,0:T(8,128)(2,1)} %copy.47) | data formatting | bytes 1048576 | tf_op jit(solution)/shard_map/concatenate | solution.py:34
  87.3 1.1 concatenate.24
  88.4 1.7 abs.31
  90.1 2.0 %fusion.16 = f32[2048,128]{1,0:T(8,128)S(1)} fusion(bf16[2048,128]{1,0:T(8,128)(2,1)} %concatenate.24, bf16[2048,128]{1,0:T(8,128)(2,1)} %abs.31, bf16[2048,128]{1,0:T(8,128)(2,1)} %concatenate.23, s32[384]{0:T(512)S(1)} %iota_add_fusion), kind=kOutput, calls=%fused_computation.27 | convolution fusion | flops 206192640 | bytes 2622976 | tf_op jit(solution)/shard_map/dot_general | solution.py:38
  92.6 0.7 copy-done.1
  93.4 2.5 %fusion.7 = f32[128,512]{1,0:T(8,128)S(1)} fusion(bf16[2048,256]{1,0:T(8,128)(2,1)} %get-tuple-element.16, bf16[2048,256]{1,0:T(8,128)(2,1)} %get-tuple-element.15, f32[128,2048]{0,1:T(8,128)S(1)} %copy-done.1, f32[128,2048]{0,1:T(8,128)S(1)} %copy.50, f32[2048]{0:T(1024)S(1)} %fusion.49), kind=kOutput, calls=%fused_computation.16 | convolution fusion | flops 273678336 | bytes 4464640 | tf_op jit(solution)/shard_map/dot_general | solution.py:74
  96.2 9.4 %all_gather.3 = bf16[2,256,512]{2,1,0:T(8,128)(2,1)S(1)} all-gather(bf16[2,64,512]{2,1,0:T(8,128)(2,1)S(1)} %bitcast.48), channel_id=1, replica_groups=mesh['chan'=64,'rep'=4] {'rep'}, dimensions={1}, use_global_device_ids=true | all-gather | bytes 655360 | tf_op jit(solution)/shard_map/all_gather | solution.py:130
  106.0 79.2 %all-reduce.2 = bf16[128,2,512]{2,0,1:T(8,128)(2,1)S(1)} all-reduce(f32[128,2,512]{2,0,1:T(8,128)S(1)} %fusion.41), channel_id=1, replica_groups=mesh['chan'=64,'rep'=4] {'chan','rep'}, use_global_device_ids=true, to_apply=%region_2.3 | all-reduce | flops 131072 | bytes 786432 | tf_op jit(solution)/shard_map/psum | solution.py:124
  185.4 1.5 add_convert_fusion
  186.9 2.7 %bitcast_divide_fusion = f32[32,64,256]{2,1,0:T(8,128)} fusion(bf16[32,64,2,256]{3,1,2,0:T(8,128)(2,1)S(1)} %get-tuple-element.10, bf16[32,64,2,256]{3,1,2,0:T(8,128)(2,1)S(1)} %get-tuple-element.9, f32[32,256]{1,0:T(8,128)S(1)} %fusion.22, bf16[2,256,512]{2,1,0:T(8,128)(2,1)S(1)} %all_gather.3), kind=kOutput, calls=%fused_computation.21 | convolution fusion | flops 1082654720 | bytes 6848512 | tf_op jit(solution)/shard_map/dot_general | solution.py:93
  (38 shorter events, 2.7 us)
Async XLA Ops:
  30.7 16.8 %copy-start.2 = (s32[128]{0:T(128)S(1)}, s32[128]{0:T(128)}, u32[]{:S(2)}) copy-start(s32[128]{0:T(128)} %param.4) | copy-start | bytes 1540
  33.6 32.1 %all-to-all-start = ((bf16[64,2,2048]{2,1,0:T(2,128)(2,1)}), bf16[64,2,2048]{2,1,0:T(2,128)(2,1)S(1)}, u32[]{:S(2)}, u32[]{:S(2)}) async-start(bf16[64,2,2048]{2,1,0:T(2,128)(2,1)} %reshape.254), calls=%async_computation | async-start | bytes 1048576 | tf_op jit(solution)/shard_map/all_to_all | solution.py:115
  78.1 3.4 %copy-start = (bf16[2,1,64,64,32]{2,0,4,3,1:T(2,128)(2,1)S(1)}, bf16[2,1,64,64,32]{2,0,4,3,1:T(2,128)(2,1)}, u32[]{:S(2)}) copy-start(bf16[2,1,64,64,32]{2,0,4,3,1:T(2,128)(2,1)} %copy.46) | copy-start | bytes 1572868
  92.1 1.2 copy-start.1
where the time goes:
time: 190 us
  blocking collectives  88.6 us (47%)
  local copies, waits for them, and re-layouts  62 us (33%)
  other arithmetic  16.8 us (9%)
  starting transfers between devices  13.8 us (7%)
  matrix products  8.04 us (4%)
    psum x1, blocking collectives, shards(): summed = lax.psum(picked, ('chan', 'rep'))  79.2 us
    gather x1, local copies, waits for them, and re-layouts, shards(): live_here = live[:, group_ids]  14.1 us
    all_to_all x1, starting transfers between devices, shards(): lax.all_to_all(masked, 'chan', split_axis=1, concat_axis=3, tiled=True)  13.8 us
    unnamed x11, local copies, waits for them, and re-layouts  11 us
    another operation x2, other arithmetic  10.9 us
    all_gather x1, blocking collectives, shards(): piece = lax.all_gather(spectra, 'rep', axis=1, tiled=True)  9.42 us
    abs x4, local copies, waits for them, and re-layouts, running_mean(): magnitude = jnp.abs(records)  8.32 us
    convert_element_type x2, local copies, waits for them, and re-layouts, preprocess(): records.astype(jnp.float32) / (mean_abs + tiny_eps)  8.27 us
  transfers between devices with their start and end apart: 1, of which 0 were waited for; matrix products, arithmetic and copies ran while one was open for 10% of the time, Pallas kernels for 0%

commit v1 on v0

--- a/solution.py
+++ b/solution.py
@@ -121,7 +121,7 @@
     onehot = (sources[:, None] == own_ids[None, :]).astype(jnp.bfloat16)
     picked = jnp.einsum("sc,wcf->swf", onehot, spectra, preferred_element_type=jnp.float32)
     quarter = sources.shape[0] // reps
-    summed = lax.psum(picked, ("chan", "rep"))
+    summed = lax.psum(lax.psum(picked, "rep"), "chan")
     mine = lax.dynamic_slice_in_dim(summed, rep_place * quarter, quarter, 0)
     source_spectrum = mine.astype(jnp.bfloat16)
     source_live = live[:, sources]

time: 190 us -> 470 us (2.47)
  the two profiles are of different devices: /device:TPU:1 before, /device:TPU:4 now
where the time goes in v1:
time: 470 us
  blocking collectives  321 us (68%)
  local copies, waits for them, and re-layouts  62.3 us (13%)
  waiting for transfers between devices  33.7 us (7%)
  other arithmetic  17 us (4%)
  between operations  13.7 us (3%)
  starting transfers between devices  12.8 us (3%)
  matrix products  8.83 us (2%)
    psum x1, blocking collectives, shards(): summed = lax.psum(lax.psum(picked, 'rep'), 'chan')  313 us
    psum x1, waiting for transfers between devices, shards(): summed = lax.psum(lax.psum(picked, 'rep'), 'chan')  29.3 us
    gather x1, local copies, waits for them, and re-layouts, shards(): live_here = live[:, group_ids]  14.1 us
    all_to_all x1, starting transfers between devices, shards(): lax.all_to_all(masked, 'chan', split_axis=1, concat_axis=3, tiled=True)  12.7 us
    unnamed x11, local copies, waits for them, and re-layouts  11 us
    another operation x2, other arithmetic  10.9 us
  transfers between devices with their start and end apart: 2, of which 2 were waited for; matrix products, arithmetic and copies ran while one was open for 4% of the time, Pallas kernels for 0%

profile of v1, /device:TPU:4, one launch (start us, length us, event | category | flops | bytes accessed | tf_op | source)
XLA Modules:
  0.0 469.5 jit_solution(15151965742052058018)
XLA Ops:
  7.2 0.8 and_reduce_fusion
  8.0 0.7 multiply_reduce_fusion
  8.9 8.1 %scatter_custom_fusion = f32[32768]{0:T(1024)S(1)} fusion(s32[2048]{0:T(1024)S(1)} %bitcast.50, f32[2048]{0:T(1024)S(1)} %broadcast.257, f32[]{:T(128)} %constant.27.clone.1), kind=kCustom, calls=%fused_computation.68 | custom fusion | bytes 131076
  17.1 5.0 %copy.42 = f32[2,16384]{0,1:T(8,128)} copy(f32[2,16384]{1,0:T(2,128)S(1)} %reshape.212) | data formatting | bytes 262144 | tf_op jit(solution)/shard_map/scatter | solution.py:22
  22.1 14.1 %gather_fusion = f32[4096,2]{1,0:T(8,128)S(1)} fusion(f32[2,16384]{0,1:T(8,128)} %copy.42, s32[4096]{0:T(1024)S(1)} %broadcast_clamp_fusion), kind=kCustom, calls=%fused_computation | custom fusion | bytes 81920 | tf_op jit(solution)/shard_map/gather | solution.py:113
  36.5 0.7 copy.43
  37.3 1.4 fusion.59
  38.6 1.5 reshape.254
  40.2 12.7 %all-to-all-start = ((bf16[64,2,2048]{2,1,0:T(2,128)(2,1)}), bf16[64,2,2048]{2,1,0:T(2,128)(2,1)S(1)}, u32[]{:S(2)}, u32[]{:S(2)}) async-start(bf16[64,2,2048]{2,1,0:T(2,128)(2,1)} %reshape.254), calls=%async_computation | async-start | bytes 1048576 | tf_op jit(solution)/shard_map/all_to_all | solution.py:115
  53.3 4.0 gather_fusion.1
  57.7 9.4 %cosine_convert_fusion = (bf16[2048,256]{1,0:T(8,128)(2,1)}, bf16[2048,256]{1,0:T(8,128)(2,1)}) fusion(s32[256]{0:T(256)S(1)} %iota_add_fusion.1), kind=kLoop, calls=%fused_computation.23 | loop fusion | flops 8912896 | bytes 2098176 | tf_op jit(solution)/shard_map/convert.5
  67.1 4.3 all-to-all-done
  72.1 1.5 abs_bitcast_fusion
  73.6 2.1 copy.46
  75.7 3.2 copy.48
  79.0 4.9 %copy.45 = f32[2,1,64,64,32]{2,0,4,3,1:T(2,128)} copy(f32[2,1,64,64,32]{2,4,0,3,1:T(8,128)} %get-tuple-element.6) | data formatting | bytes 2097152 | tf_op jit(solution)/shard_map/convert_element_type | solution.py:73
  83.9 3.4 reshape.213
  87.3 1.3 abs.30
  88.6 1.3 pad_slice_fusion.1
  89.9 1.1 copy.47
  91.0 2.1 concatenate.23
  93.3 1.1 concatenate.24
  94.4 1.7 abs.31
  96.2 2.0 fusion.16
  99.4 2.5 fusion.7
  102.3 1.1 fusion.41
  103.4 4.1 gather_fusion.2
  107.8 8.4 %all_gather.3 = bf16[2,256,512]{2,1,0:T(8,128)(2,1)S(1)} all-gather(bf16[2,64,512]{2,1,0:T(8,128)(2,1)S(1)} %bitcast.49), channel_id=1, replica_groups=mesh['chan'=64,'rep'=4] {'rep'}, dimensions={1}, use_global_device_ids=true | all-gather | bytes 655360 | tf_op jit(solution)/shard_map/all_gather | solution.py:130
  116.2 29.3 %all-reduce.4.cloned.1.call-done = f32[128,2,512]{2,0,1:T(8,128)} async-done(((f32[128,2,512]{2,0,1:T(8,128)}), f32[128,2,512]{2,0,1:T(8,128)}) %all-reduce.4.cloned.1.call-update) | async-done | bytes 524304 | tf_op jit(solution)/shard_map/psum | solution.py:124
  145.5 312.8 %all-reduce.5 = bf16[128,2,512]{2,0,1:T(8,128)(2,1)S(1)} all-reduce(f32[128,2,512]{2,0,1:T(8,128)} %all-reduce.4.cloned.1.call-done), channel_id=1, replica_groups=mesh['chan'=64,'rep'=4] {'chan'}, use_global_device_ids=true, to_apply=%region_3.4 | all-reduce | flops 131072 | bytes 786432 | tf_op jit(solution)/shard_map/psum | solution.py:124
  458.5 1.5 add_convert_fusion
  460.0 2.7 bitcast_divide_fusion
  (41 shorter events, 4.7 us)
Async XLA Ops:
  37.2 16.0 %copy-start.2 = (s32[128]{0:T(128)S(1)}, s32[128]{0:T(128)}, u32[]{:S(2)}) copy-start(s32[128]{0:T(128)} %param.4) | copy-start | bytes 1540
  40.2 31.2 %all-to-all-start = ((bf16[64,2,2048]{2,1,0:T(2,128)(2,1)}), bf16[64,2,2048]{2,1,0:T(2,128)(2,1)S(1)}, u32[]{:S(2)}, u32[]{:S(2)}) async-start(bf16[64,2,2048]{2,1,0:T(2,128)(2,1)} %reshape.254), calls=%async_computation | async-start | bytes 1048576 | tf_op jit(solution)/shard_map/all_to_all | solution.py:115
  52.9 92.6 %all-reduce.4.cloned.1.call-start = ((), (), s32[]{:S(2)}) async-start(), calls=%async_computation.1 | async-start | bytes 1048576 | tf_op jit(solution)/shard_map/psum | solution.py:124
  83.9 3.4 copy-start
  98.2 1.2 copy-start.1
Sparse Core Ops, SparseCore 0:
  103.5 41.8 all-reduce.3
